TPU v7x, 128 devices: a whole 4x4x4 slice. The times are simulated.
128 devices in a mesh: row: 16 (over z, y), col: 8 (over x, core).
Axes of the slice: x: 4, y: 4, z: 4, core: 2. Of those that a mesh axis runs over, the one named last changes fastest.
Arguments:
- hidden: bfloat16 [4096, 8192], P('row', 'col'), may hold values from -96 to 96
- norm_gain: bfloat16 [8192], P('col'), may hold values from 0.5 to 1.5
- w_query: bfloat16 [8192, 4096], P('row', 'col')
- w_key: bfloat16 [8192, 4096], P('row', 'col')
- w_value: bfloat16 [8192, 4096], P('row', 'col'), may hold values from -0.0625 to 0.0625
- w_out: bfloat16 [4096, 8192], P('row', 'col'), may hold values from -0.09375 to 0.09375
Outputs:
- context: bfloat16 [4096, 4096], P('row', 'col')
- layer_out: bfloat16 [4096, 8192], P('row', 'col')
All inputs are finite; a program needn't handle non-finite values.
Results may differ from a plain program's by a relative error of at most 0.04.
Values may be sent and summed in bfloat16 or wider, within the bound.
A program may use at most 128 MiB of HBM per device.

v0:
```python
import math
import jax
import jax.numpy as jnp
from jax import lax
from jax.sharding import PartitionSpec as P

HD = 128
norm_epsilon = 1e-05


def rows_first(arrays, axis, dims):
    turned = [jnp.moveaxis(a, dim, 0) for a, dim in zip(arrays, dims)]
    widths = [t[0].size for t in turned]
    both = jnp.concatenate([t.reshape(-1, w) for t, w in zip(turned, widths)], axis=1)
    result = lax.all_gather(both, axis, axis=0, tiled=True)
    parts = jnp.split(result, [sum(widths[:k]) for k in range(1, len(widths))], axis=1)
    return tuple(
        (
            jnp.moveaxis(b.reshape(-1, *t.shape[1:]), 0, dim)
            for b, t, dim in zip(parts, turned, dims)
        )
    )


def side_by_side(arrays, axis, dim, along):
    widths = [a.shape[along] for a in arrays]
    both = jnp.concatenate(arrays, axis=along)
    result = lax.all_gather(both, axis, axis=dim, tiled=True)
    return tuple(jnp.split(result, [sum(widths[:k]) for k in range(1, len(widths))], axis=along))


def laid_out(parts, dim):
    parts = jnp.moveaxis(parts, 0, dim)
    lengths = parts.shape
    return parts.reshape(*lengths[:dim], lengths[dim] * lengths[dim + 1], *lengths[dim + 2 :])


def from_everyone(shard, axis):
    size = lax.axis_size(axis)
    return lax.all_to_all(
        jnp.broadcast_to(shard[None], (size, *shard.shape)), axis, 0, 0, tiled=True
    )


def gather_directly(shard, axis, dim):
    return laid_out(from_everyone(shard, axis), dim)


def rotary(values, positions):
    half = values.shape[-1] // 2
    freqs = jnp.exp(
        -math.log(10000.0) * 2.0 * jnp.arange(half, dtype=jnp.float32) / values.shape[-1]
    )
    angles = positions.astype(jnp.float32)[:, None] * freqs[None, :]
    cosine = jnp.cos(angles)[:, None, :]
    sine = jnp.sin(angles)[:, None, :]
    first = values[..., :half]
    second = values[..., half:]
    return jnp.concatenate(
        (first * cosine - second * sine, second * cosine + first * sine), axis=-1
    )


def blocked_sum(left, piece, block):
    count = piece.shape[0] // block
    split_left = left.reshape(left.shape[0], count, block)
    split_right = piece.reshape(count, block, piece.shape[1])
    terms = jnp.einsum("tbk,bkf->btf", split_left, split_right, preferred_element_type=jnp.float32)
    rounded = lax.optimization_barrier(terms.astype(jnp.bfloat16))
    return jnp.sum(rounded.astype(jnp.float32), axis=0)


def attend(carry, keys, values, queries, query_positions, key_positions, scale):
    peak, total, weighted = carry
    scores = jnp.einsum("qhd,khd->hqk", queries, keys, preferred_element_type=jnp.float32) * scale
    allowed = key_positions[None, :] <= query_positions[:, None]
    scores = jnp.where(allowed[None, :, :], scores, -jnp.inf)
    new_peak = jnp.maximum(peak, jnp.max(scores, axis=2))
    probs = jnp.exp(scores - new_peak[:, :, None])
    total = jnp.sum(probs, axis=2)
    weighted = jnp.einsum(
        "hqk,khd->hqd", probs.astype(jnp.bfloat16), values, preferred_element_type=jnp.float32
    )
    return (new_peak, total, weighted)


def start_state(heads_here, count):
    return (
        jnp.full((heads_here, count), -1e30, jnp.float32),
        jnp.zeros((heads_here, count), jnp.float32),
        jnp.zeros((heads_here, count, HD), jnp.float32),
    )


def finish(carry, count, heads_here):
    peak, total, weighted = carry
    return (
        (weighted / total[:, :, None])
        .transpose(1, 0, 2)
        .reshape(count, heads_here * HD)
        .astype(jnp.bfloat16)
    )


def on_device(hidden, norm_gain, w_query, w_key, w_value, w_out):
    rows = hidden.shape[0]
    residual = hidden.astype(jnp.float32)
    whole, gains = rows_first((hidden, norm_gain), "col", (1, 0))
    wide_rows = whole.astype(jnp.float32)
    mean_square = jnp.mean(wide_rows * wide_rows, axis=1, keepdims=True)
    normed = (
        wide_rows * lax.rsqrt(mean_square + norm_epsilon) * gains.astype(jnp.float32)[None, :]
    ).astype(jnp.bfloat16)
    block = w_query.shape[0]
    pieces = side_by_side((w_query, w_key, w_value), "row", 0, 1)
    segment = normed
    proj_q, proj_k, proj_v = tuple((blocked_sum(segment, piece, block) for piece in pieces))
    heads_here = w_query.shape[1] // HD
    row_index = lax.axis_index("row")
    first_row = row_index * rows
    positions = first_row + jnp.arange(rows, dtype=jnp.int32)
    query = rotary(proj_q.reshape(rows, heads_here, HD), positions).astype(jnp.bfloat16)
    keys_here = (
        rotary(proj_k.reshape(rows, heads_here, HD), positions)
        .astype(jnp.bfloat16)
        .reshape(rows, heads_here * HD)
    )
    values_here = proj_v.astype(jnp.bfloat16)
    scale = 1.0 / math.sqrt(HD)
    initial = start_state(heads_here, rows)
    pieces = side_by_side((keys_here, values_here), "row", 0, 1)
    keys = pieces[0].reshape(-1, heads_here, HD)
    values = pieces[1].reshape(-1, heads_here, HD)
    key_positions = jnp.arange(keys.shape[0], dtype=jnp.int32)
    folded = attend(initial, keys, values, query, positions, key_positions, scale)
    context = finish(folded, rows, heads_here)
    gathered_context = gather_directly(context, "col", 1)
    out_block = w_out.shape[0]
    segment = gathered_context
    attended = blocked_sum(segment, lax.all_gather(w_out, "row", axis=0, tiled=True), out_block)
    layer_out = (residual + attended).astype(jnp.bfloat16)
    return (context, layer_out)


def solution(mesh):
    placed = (
        P("row", "col"),
        P("col"),
        P("row", "col"),
        P("row", "col"),
        P("row", "col"),
        P("row", "col"),
    )
    return jax.shard_map(
        on_device,
        mesh=mesh,
        in_specs=placed,
        out_specs=(P("row", "col"), P("row", "col")),
        check_vma=False,
    )
```

profile of v0, /device:TPU:1, one launch (start us, length us, event | category | flops | bytes accessed | tf_op | source)
XLA Modules:
  0.0 393.5 jit_solution(4112995521757961650)
XLA Ops:
  7.9 1.9 pad_maximum_fusion.1
  9.8 2.6 pad_maximum_fusion
  12.6 1.2 multiply_cosine_fusion
  13.8 32.3 %all-gather.5.cloned.1.call-done = bf16[8192,257]{0,1:T(8,128)(2,1)} async-done(((bf16[1024,257]{0,1:T(8,128)(2,1)}), bf16[8192,257]{0,1:T(8,128)(2,1)}) %all-gather.5.cloned.1.call-update) | async-done | bytes 4210704 | tf_op jit(solution)/shard_map/all_gather | solution.py:15
  46.1 3.1 fusion.3
  50.1 5.4 %fusion.5 = bf16[8192,256]{0,1:T(8,128)(2,1)} fusion(f32[8192]{0:T(1024)S(1)} %bitcast.60, f32[256]{0:T(256)S(1)} %add_rsqrt_fusion, bf16[8192,257]{0,1:T(8,128)(2,1)} %all-gather.5.cloned.1.call-done), kind=kLoop, calls=%fused_computation.10 | loop fusion | flops 8388608 | bytes 8422400 | tf_op jit(solution)/shard_map/convert_element_type | solution.py:113
  55.6 146.4 %all-gather.7.cloned.1.call-done = bf16[8192,1536]{1,0:T(8,128)(2,1)} async-done(((bf16[512,1536]{1,0:T(8,128)(2,1)}), bf16[8192,1536]{1,0:T(8,128)(2,1)}) %all-gather.7.cloned.1.call-update) | async-done | bytes 25165840 | tf_op jit(solution)/shard_map/all_gather | solution.py:28
  201.9 12.4 %fusion.44 = (bf16[8192,512]{1,0:T(8,128)(2,1)S(1)}, bf16[8192,512]{1,0:T(8,128)(2,1)S(1)}, bf16[8192,512]{1,0:T(8,128)(2,1)}) fusion(bf16[8192,1536]{1,0:T(8,128)(2,1)} %all-gather.7.cloned.1.call-done), kind=kLoop, calls=%fused_computation.56 | loop fusion | bytes 50331648 | tf_op jit(solution)/shard_map/split | solution.py:29
  214.3 4.3 %fusion.24 = bf16[16,256,512]{2,1,0:T(8,128)(2,1)} fusion(bf16[16,512,512]{2,1,0:T(8,128)(2,1)S(1)} %bitcast.49, bf16[32,16,8,512]{3,2,1,0:T(8,128)(2,1)S(1)} %bitcast.51), kind=kOutput, calls=%fused_computation.28 | convolution fusion | flops 2149580800 | bytes 16777216 | tf_op jit(solution)/shard_map/tbk,bkf->btf/dot_general | solution.py:68
  218.6 2.3 fusion.18
  222.2 7.0 %fusion.21 = bf16[16,256,512]{2,1,0:T(8,128)(2,1)S(1)} fusion(bf16[16,512,512]{2,1,0:T(8,128)(2,1)} %bitcast.47, bf16[32,16,8,512]{3,2,1,0:T(8,128)(2,1)} %bitcast.50), kind=kOutput, calls=%fused_computation.27 | convolution fusion | flops 2149580800 | bytes 16777216 | tf_op jit(solution)/shard_map/tbk,bkf->btf/dot_general | solution.py:68
  231.2 2.8 reduce_sum.60
  236.2 69.4 %all-gather.9.cloned.1.call-done = bf16[4096,1024]{1,0:T(8,128)(2,1)} async-done(((bf16[256,1024]{1,0:T(8,128)(2,1)}), bf16[4096,1024]{1,0:T(8,128)(2,1)}) %all-gather.9.cloned.1.call-update) | async-done | bytes 8388624 | tf_op jit(solution)/shard_map/all_gather | solution.py:28
  305.6 5.7 %fusion.45 = (bf16[4096,512]{1,0:T(8,128)(2,1)}, bf16[4096,512]{1,0:T(8,128)(2,1)}) fusion(bf16[4096,1024]{1,0:T(8,128)(2,1)} %all-gather.9.cloned.1.call-done), kind=kLoop, calls=%fused_computation.57 | loop fusion | bytes 16777216 | tf_op jit(solution)/shard_map/split | solution.py:29
  311.4 6.4 %copy.37 = bf16[4096,512]{0,1:T(8,128)(2,1)} copy(bf16[4096,512]{1,0:T(8,128)(2,1)} %get-tuple-element.12) | data formatting | bytes 8388608 | tf_op jit(solution)/shard_map/split | solution.py:29
  317.8 6.4 %copy.35 = bf16[4096,512]{0,1:T(8,128)(2,1)} copy(bf16[4096,512]{1,0:T(8,128)(2,1)} %get-tuple-element.11) | data formatting | bytes 8388608 | tf_op jit(solution)/shard_map/split | solution.py:29
  324.2 5.8 %fusion = (f32[4,256]{1,0:T(4,128)S(1)}, f32[4,256,4096]{2,1,0:T(8,128)S(1)}) fusion(pred[256,4096]{1,0:T(8,128)(4,1)S(1)} %iota_compare_fusion, bf16[4096,4,128]{0,2,1:T(8,128)(2,1)} %bitcast.44, bf16[256,4,64]{2,0,1:T(8,128)(2,1)S(1)} %get-tuple-element.14, bf16[256,4,64]{2,0,1:T(8,128)(2,1)S(1)} %get-tuple-element.13), kind=kOutput, calls=%fused_computation.3 | convolution fusion | flops 1086848000 | bytes 22286336 | tf_op jit(solution)/shard_map/qhd,khd->hqk/dot_general | solution.py:75
  330.0 4.4 %fusion.1 = f32[4,256]{1,0:T(4,128)S(1)} fusion(f32[4,256,4096]{2,1,0:T(8,128)S(1)} %get-tuple-element.26, f32[4,256]{1,0:T(4,128)S(1)} %broadcast_maximum_fusion, pred[256,4096]{1,0:T(8,128)(4,1)S(1)} %iota_compare_fusion), kind=kLoop, calls=%fused_computation.4 | loop fusion | flops 16776192 | bytes 17833984 | tf_op jit(solution)/shard_map/reduce_sum | solution.py:80
  334.5 6.7 %fusion.33 = bf16[256,4,128]{0,2,1:T(8,128)(2,1)S(1)} fusion(bf16[4096,4,128]{0,2,1:T(8,128)(2,1)} %bitcast.53, f32[4,256,4096]{2,1,0:T(8,128)S(1)} %get-tuple-element.26, f32[4,256]{1,0:T(4,128)S(1)} %broadcast_maximum_fusion, pred[256,4096]{1,0:T(8,128)(4,1)S(1)} %iota_compare_fusion, f32[256,4]{0,1:T(4,128)S(1)} %bitcast.61), kind=kOutput, calls=%fused_computation.33 | convolution fusion | flops 1090781184 | bytes 22290432 | tf_op jit(solution)/shard_map/hqk,khd->hqd/dot_general | solution.py:81
  341.1 1.5 broadcast_in_dim.15
  342.6 5.2 %all-to-all-start = ((bf16[8,256,512]{1,2,0:T(8,128)(2,1)}), bf16[8,256,512]{1,2,0:T(8,128)(2,1)S(1)}, u32[]{:S(2)}, u32[]{:S(2)}) async-start(bf16[8,256,512]{1,2,0:T(8,128)(2,1)} %broadcast_in_dim.15), calls=%async_computation | async-start | bytes 4194304 | tf_op jit(solution)/shard_map/all_to_all | solution.py:40
  348.7 29.5 %all-gather.11.cloned.1.call-done = bf16[4096,1024]{1,0:T(8,128)(2,1)} async-done(((bf16[256,1024]{1,0:T(8,128)(2,1)}), bf16[4096,1024]{1,0:T(8,128)(2,1)}) %all-gather.11.cloned.1.call-update) | async-done | bytes 8388624 | tf_op jit(solution)/shard_map/all_gather | solution.py:140
  378.2 5.8 %convolution_convert_fusion = bf16[16,256,1024]{2,1,0:T(8,128)(2,1)S(1)} fusion(bf16[256,16,256]{0,2,1:T(8,128)(2,1)S(1)} %bitcast.45, bf16[16,256,1024]{2,1,0:T(8,128)(2,1)} %bitcast.46), kind=kOutput, calls=%fused_computation.15 | convolution fusion | flops 2151677952 | bytes 18874368 | tf_op jit(solution)/shard_map/tbk,bkf->btf/dot_general | solution.py:68
  384.0 2.0 convert_reduce_fusion
  (41 shorter events, 8.8 us)
Async XLA Ops:
  7.2 38.9 %all-gather.5.cloned.1.call-start = ((), (), s32[]{:S(2)}) async-start(), calls=%async_computation.1 | async-start | bytes 4866048 | tf_op jit(solution)/shard_map/all_gather | solution.py:15
  9.8 192.1 %all-gather.7.cloned.1.call-start = ((), (), s32[]{:S(2)}) async-start(), calls=%async_computation.2 | async-start | bytes 26738688 | tf_op jit(solution)/shard_map/all_gather | solution.py:28
  12.5 293.2 %all-gather.9.cloned.1.call-start = ((), (), s32[]{:S(2)}) async-start(), calls=%async_computation.3 | async-start | bytes 8912896 | tf_op jit(solution)/shard_map/all_gather | solution.py:28
  201.9 12.4 %copy-start = (bf16[8192,256]{0,1:T(8,128)(2,1)S(1)}, bf16[8192,256]{0,1:T(8,128)(2,1)}, u32[]{:S(2)}) copy-start(bf16[8192,256]{0,1:T(8,128)(2,1)} %fusion.5) | copy-start | bytes 12582916
  229.2 1.3 copy-start.2
  229.2 1.3 copy-start.3
  235.0 143.2 %all-gather.11.cloned.1.call-start = ((), (), s32[]{:S(2)}) async-start(), calls=%async_computation.4 | async-start | bytes 8912896 | tf_op jit(solution)/shard_map/all_gather | solution.py:140
  342.6 35.5 %all-to-all-start = ((bf16[8,256,512]{1,2,0:T(8,128)(2,1)}), bf16[8,256,512]{1,2,0:T(8,128)(2,1)S(1)}, u32[]{:S(2)}, u32[]{:S(2)}) async-start(bf16[8,256,512]{1,2,0:T(8,128)(2,1)} %broadcast_in_dim.15), calls=%async_computation | async-start | bytes 4194304 | tf_op jit(solution)/shard_map/all_to_all | solution.py:40
  384.0 2.0 copy-start.1
Sparse Core Ops, SparseCore 0:
  9.9 36.1 all-gather.4
  48.2 153.6 all-gather.6
  235.1 70.5 all-gather.8
  307.6 70.5 all-gather.10
where the time goes:
time: 394 us; the launch traced here: 393 us
  waiting for transfers between devices  278 us (71%)
  local copies, waits for them, and re-layouts  35.5 us (9%)
  matrix products  31.9 us (8%)
  other arithmetic  28.6 us (7%)
  between operations  14 us (4%)
  starting transfers between devices  5.33 us (1%)
    all_gather x2, waiting for transfers between devices, side_by_side(): result = lax.all_gather(both, axis, axis=dim, tiled=True)  216 us
    all_gather x1, waiting for transfers between devices, rows_first(): result = lax.all_gather(both, axis, axis=0, tiled=True)  32.3 us
    split x4, local copies, waits for them, and re-layouts, side_by_side(): jnp.split(result, [sum(widths[:k]) for k in range(1, len(widths))], axis=...  31 us
    all_gather x1, waiting for transfers between devices, on_device(): lax.all_gather(w_out, 'row', axis=0, tiled=True)  29.5 us
    dot_general x4, matrix products, blocked_sum(): jnp.einsum('tbk,bkf->btf', split_left, split_right, preferred_element_typ...  19.4 us
  transfers between devices with their start and end apart: 5, of which 4 were waited for; matrix products, arithmetic and copies ran while one was open for 13% of the time, Pallas kernels for 0%

commit v1 on v0

--- a/solution.py
+++ b/solution.py
@@ -12,7 +12,10 @@
     turned = [jnp.moveaxis(a, dim, 0) for a, dim in zip(arrays, dims)]
     widths = [t[0].size for t in turned]
     both = jnp.concatenate([t.reshape(-1, w) for t, w in zip(turned, widths)], axis=1)
-    result = lax.all_gather(both, axis, axis=0, tiled=True)
+    count_2 = lax.axis_size(axis)
+    blocks = jnp.stack([both for _ in range(count_2)])
+    blocks = lax.all_to_all(blocks, axis, split_axis=0, concat_axis=0)
+    result = jnp.concatenate(blocks, axis=0)
     parts = jnp.split(result, [sum(widths[:k]) for k in range(1, len(widths))], axis=1)
     return tuple(
         (

time: 394 us -> 372 us (0.944)
  waiting for transfers between devices: 278 us -> 230 us
  local copies, waits for them, and re-layouts: 35.5 us -> 48.9 us
  matrix products: 31.9 us -> 38.7 us
  starting transfers between devices: 5.33 us -> 11 us
    all_gather x2, waiting for transfers between devices: 216 us -> 150 us  [side_by_side(): result = lax.all_gather(both, axis, axis=dim, tiled=True)]
    all_to_all x0 -> x1, waiting for transfers between devices: none -> 49.7 us  [rows_first(): blocks = lax.all_to_all(blocks, axis, split_axis=0, concat_axis=0)]
    all_gather x1 -> x0, waiting for transfers between devices: 32.3 us -> none  [rows_first(): result = lax.all_gather(both, axis, axis=0, tiled=True)]
    all_to_all x0 -> x1, local copies, waits for them, and re-layouts: none -> 7.88 us  [rows_first(): blocks = lax.all_to_all(blocks, axis, split_axis=0, concat_axis=0)]
    dot_general x4, matrix products: 19.4 us -> 26.2 us  [blocked_sum(): jnp.einsum('tbk,bkf->btf', split_left, split_right, preferred_element_typ...]
    all_to_all x0 -> x1, starting transfers between devices: none -> 5.84 us  [rows_first(): blocks = lax.all_to_all(blocks, axis, split_axis=0, concat_axis=0)]
  transfers between devices with their start and end apart: 5 -> 5, of which waited for: 4 -> 4; matrix products, arithmetic and copies ran while one was open for 13% -> 16% of each run, Pallas kernels for 0% -> 0%
where the time goes in v1:
time: 372 us; the launch traced here: 371 us
  waiting for transfers between devices  230 us (62%)
  local copies, waits for them, and re-layouts  48.9 us (13%)
  matrix products  38.7 us (10%)
  other arithmetic  28.2 us (8%)
  between operations  13.9 us (4%)
  starting transfers between devices  11 us (3%)
    all_gather x2, waiting for transfers between devices, side_by_side(): result = lax.all_gather(both, axis, axis=dim, tiled=True)  150 us
    all_to_all x1, waiting for transfers between devices, rows_first(): blocks = lax.all_to_all(blocks, axis, split_axis=0, concat_axis=0)  49.7 us
    split x4, local copies, waits for them, and re-layouts, side_by_side(): jnp.split(result, [sum(widths[:k]) for k in range(1, len(widths))], axis=...  33.2 us
    all_gather x1, waiting for transfers between devices, on_device(): lax.all_gather(w_out, 'row', axis=0, tiled=True)  29.8 us
    dot_general x4, matrix products, blocked_sum(): jnp.einsum('tbk,bkf->btf', split_left, split_right, preferred_element_typ...  26.2 us
    reduce_sum x4, other arithmetic, blocked_sum(): return jnp.sum(rounded.astype(jnp.float32), axis=0)  8.26 us
    all_to_all x1, local copies, waits for them, and re-layouts, rows_first(): blocks = lax.all_to_all(blocks, axis, split_axis=0, concat_axis=0)  7.88 us
  transfers between devices with their start and end apart: 5, of which 4 were waited for; matrix products, arithmetic and copies ran while one was open for 16% of the time, Pallas kernels for 0%

profile of v1, /device:TPU:1, one launch (start us, length us, event | category | flops | bytes accessed | tf_op | source)
XLA Modules:
  0.0 371.0 jit_solution(17740609961970122112)
XLA Ops:
  7.2 2.6 pad_maximum_fusion
  11.6 2.6 stack.2
  14.2 5.8 %all-to-all-start = ((bf16[8,1024,257]{1,2,0:T(8,128)(2,1)}), bf16[8,1024,257]{1,2,0:T(8,128)(2,1)}, u32[]{:S(2)}, u32[]{:S(2)}) async-start(bf16[8,1024,257]{1,2,0:T(8,128)(2,1)} %stack.2), calls=%async_computation | async-start | bytes 8650752 | tf_op jit(solution)/shard_map/all_to_all | solution.py:17
  20.6 49.7 %all-to-all-done = bf16[8,1024,257]{1,2,0:T(8,128)(2,1)} async-done(((bf16[8,1024,257]{1,2,0:T(8,128)(2,1)}), bf16[8,1024,257]{1,2,0:T(8,128)(2,1)}, u32[]{:S(2)}, u32[]{:S(2)}) %all-to-all-start) | async-done | bytes 4210720 | tf_op jit(solution)/shard_map/all_to_all | solution.py:17
  70.2 7.9 %copy.23 = bf16[8,1024,257]{2,1,0:T(8,128)(2,1)} copy(bf16[8,1024,257]{1,2,0:T(8,128)(2,1)} %all-to-all-done) | data formatting | bytes 8421376 | tf_op jit(solution)/shard_map/all_to_all | solution.py:17
  78.1 3.5 fusion.3
  83.9 2.6 fusion.5
  86.5 80.9 %all-gather.4.cloned.1.call-done = bf16[8192,1536]{1,0:T(8,128)(2,1)} async-done(((bf16[512,1536]{1,0:T(8,128)(2,1)}), bf16[8192,1536]{1,0:T(8,128)(2,1)}) %all-gather.4.cloned.1.call-update) | async-done | bytes 25165840 | tf_op jit(solution)/shard_map/all_gather | solution.py:31
  167.4 14.7 %fusion.26 = (bf16[8192,512]{1,0:T(8,128)(2,1)S(1)}, bf16[8192,512]{1,0:T(8,128)(2,1)}, bf16[8192,512]{1,0:T(8,128)(2,1)}) fusion(bf16[8192,1536]{1,0:T(8,128)(2,1)} %all-gather.4.cloned.1.call-done), kind=kLoop, calls=%fused_computation.47 | loop fusion | bytes 50331648 | tf_op jit(solution)/shard_map/split | solution.py:32
  182.7 4.3 %convolution_convert_fusion.3 = bf16[16,256,512]{2,1,0:T(8,128)(2,1)} fusion(bf16[256,16,512]{0,2,1:T(8,128)(2,1)S(1)} %bitcast.37, bf16[16,512,512]{2,1,0:T(8,128)(2,1)S(1)} %bitcast.43), kind=kOutput, calls=%fused_computation.20 | convolution fusion | flops 2149580800 | bytes 16777216 | tf_op jit(solution)/shard_map/tbk,bkf->btf/dot_general | solution.py:71
  187.0 2.8 convert_reduce_fusion.2
  190.5 7.0 %convolution_convert_fusion.2 = bf16[16,256,512]{2,1,0:T(8,128)(2,1)S(1)} fusion(bf16[256,16,512]{0,2,1:T(8,128)(2,1)} %bitcast.35, bf16[16,512,512]{2,1,0:T(8,128)(2,1)} %bitcast.42), kind=kOutput, calls=%fused_computation.19 | convolution fusion | flops 2149580800 | bytes 16777216 | tf_op jit(solution)/shard_map/tbk,bkf->btf/dot_general | solution.py:71
  199.5 9.1 %convolution_convert_fusion.1 = bf16[16,256,512]{2,1,0:T(8,128)(2,1)} fusion(bf16[256,16,512]{0,2,1:T(8,128)(2,1)} %bitcast.36, bf16[16,512,512]{2,1,0:T(8,128)(2,1)} %bitcast.41), kind=kOutput, calls=%fused_computation.18 | convolution fusion | flops 2149580800 | bytes 16777216 | tf_op jit(solution)/shard_map/tbk,bkf->btf/dot_general | solution.py:71
  208.6 2.8 reduce_sum.60
  213.8 69.3 %all-gather.6.cloned.1.call-done = bf16[4096,1024]{1,0:T(8,128)(2,1)} async-done(((bf16[256,1024]{1,0:T(8,128)(2,1)}), bf16[4096,1024]{1,0:T(8,128)(2,1)}) %all-gather.6.cloned.1.call-update) | async-done | bytes 8388624 | tf_op jit(solution)/shard_map/all_gather | solution.py:31
  283.0 5.7 %fusion.27 = (bf16[4096,512]{1,0:T(8,128)(2,1)}, bf16[4096,512]{1,0:T(8,128)(2,1)}) fusion(bf16[4096,1024]{1,0:T(8,128)(2,1)} %all-gather.6.cloned.1.call-done), kind=kLoop, calls=%fused_computation.48 | loop fusion | bytes 16777216 | tf_op jit(solution)/shard_map/split | solution.py:32
  288.7 6.4 %copy.35 = bf16[4096,512]{0,1:T(8,128)(2,1)} copy(bf16[4096,512]{1,0:T(8,128)(2,1)} %get-tuple-element.11) | data formatting | bytes 8388608 | tf_op jit(solution)/shard_map/split | solution.py:32
  295.2 6.4 %copy.37 = bf16[4096,512]{0,1:T(8,128)(2,1)} copy(bf16[4096,512]{1,0:T(8,128)(2,1)} %get-tuple-element.12) | data formatting | bytes 8388608 | tf_op jit(solution)/shard_map/split | solution.py:32
  301.6 5.8 %fusion = (f32[4,256]{1,0:T(4,128)S(1)}, f32[4,256,4096]{2,1,0:T(8,128)S(1)}) fusion(pred[256,4096]{1,0:T(8,128)(4,1)S(1)} %iota_compare_fusion, bf16[4096,4,128]{0,2,1:T(8,128)(2,1)} %bitcast.44, bf16[256,4,64]{2,0,1:T(8,128)(2,1)S(1)} %get-tuple-element.14, bf16[256,4,64]{2,0,1:T(8,128)(2,1)S(1)} %get-tuple-element.13), kind=kOutput, calls=%fused_computation.3 | convolution fusion | flops 1086848000 | bytes 22286336 | tf_op jit(solution)/shard_map/qhd,khd->hqk/dot_general | solution.py:78
  307.4 4.4 %fusion.1 = f32[4,256]{1,0:T(4,128)S(1)} fusion(f32[4,256,4096]{2,1,0:T(8,128)S(1)} %get-tuple-element.26, f32[4,256]{1,0:T(4,128)S(1)} %broadcast_maximum_fusion, pred[256,4096]{1,0:T(8,128)(4,1)S(1)} %iota_compare_fusion), kind=kLoop, calls=%fused_computation.4 | loop fusion | flops 16776192 | bytes 17833984 | tf_op jit(solution)/shard_map/reduce_sum | solution.py:83
  311.8 6.7 %fusion.15 = bf16[256,4,128]{0,2,1:T(8,128)(2,1)S(1)} fusion(bf16[4096,4,128]{0,2,1:T(8,128)(2,1)} %bitcast.47, f32[4,256,4096]{2,1,0:T(8,128)S(1)} %get-tuple-element.26, f32[4,256]{1,0:T(4,128)S(1)} %broadcast_maximum_fusion, pred[256,4096]{1,0:T(8,128)(4,1)S(1)} %iota_compare_fusion, f32[256,4]{0,1:T(4,128)S(1)} %bitcast.54), kind=kOutput, calls=%fused_computation.25 | convolution fusion | flops 1090781184 | bytes 22290432 | tf_op jit(solution)/shard_map/hqk,khd->hqd/dot_general | solution.py:84
  320.0 5.1 %all-to-all-start.1 = ((bf16[8,256,512]{1,2,0:T(8,128)(2,1)}), bf16[8,256,512]{1,2,0:T(8,128)(2,1)S(1)}, u32[]{:S(2)}, u32[]{:S(2)}) async-start(bf16[8,256,512]{1,2,0:T(8,128)(2,1)} %broadcast_in_dim.15), calls=%async_computation.1 | async-start | bytes 4194304 | tf_op jit(solution)/shard_map/all_to_all | solution.py:43
  326.0 29.8 %all-gather.8.cloned.1.call-done = bf16[4096,1024]{1,0:T(8,128)(2,1)} async-done(((bf16[256,1024]{1,0:T(8,128)(2,1)}), bf16[4096,1024]{1,0:T(8,128)(2,1)}) %all-gather.8.cloned.1.call-update) | async-done | bytes 8388624 | tf_op jit(solution)/shard_map/all_gather | solution.py:143
  355.7 5.8 %convolution_convert_fusion = bf16[16,256,1024]{2,1,0:T(8,128)(2,1)S(1)} fusion(bf16[256,16,256]{0,2,1:T(8,128)(2,1)S(1)} %bitcast.45, bf16[16,256,1024]{2,1,0:T(8,128)(2,1)} %bitcast.46), kind=kOutput, calls=%fused_computation.15 | convolution fusion | flops 2151677952 | bytes 18874368 | tf_op jit(solution)/shard_map/tbk,bkf->btf/dot_general | solution.py:71
  (40 shorter events, 15.3 us)
Async XLA Ops:
  7.2 160.2 %all-gather.4.cloned.1.call-start = ((), (), s32[]{:S(2)}) async-start(), calls=%async_computation.2 | async-start | bytes 26738688 | tf_op jit(solution)/shard_map/all_gather | solution.py:31
  14.2 56.1 %all-to-all-start = ((bf16[8,1024,257]{1,2,0:T(8,128)(2,1)}), bf16[8,1024,257]{1,2,0:T(8,128)(2,1)}, u32[]{:S(2)}, u32[]{:S(2)}) async-start(bf16[8,1024,257]{1,2,0:T(8,128)(2,1)} %stack.2), calls=%async_computation | async-start | bytes 8650752 | tf_op jit(solution)/shard_map/all_to_all | solution.py:17
  20.0 263.0 %all-gather.6.cloned.1.call-start = ((), (), s32[]{:S(2)}) async-start(), calls=%async_computation.3 | async-start | bytes 8912896 | tf_op jit(solution)/shard_map/all_gather | solution.py:31
  78.1 5.8 %copy-start.1 = (bf16[8,1024,257]{2,1,0:T(8,128)(2,1)S(1)}, bf16[8,1024,257]{2,1,0:T(8,128)(2,1)}, u32[]{:S(2)}) copy-start(bf16[8,1024,257]{2,1,0:T(8,128)(2,1)} %copy.23) | copy-start | bytes 12632068
  167.4 15.3 %copy-start = (bf16[8192,256]{1,0:T(8,128)(2,1)S(1)}, bf16[8192,256]{1,0:T(8,128)(2,1)}, u32[]{:S(2)}) copy-start(bf16[8192,256]{1,0:T(8,128)(2,1)} %fusion.5) | copy-start | bytes 12582916
  212.4 143.4 %all-gather.8.cloned.1.call-start = ((), (), s32[]{:S(2)}) async-start(), calls=%async_computation.4 | async-start | bytes 8912896 | tf_op jit(solution)/shard_map/all_gather | solution.py:143
  320.0 35.7 %all-to-all-start.1 = ((bf16[8,256,512]{1,2,0:T(8,128)(2,1)}), bf16[8,256,512]{1,2,0:T(8,128)(2,1)S(1)}, u32[]{:S(2)}, u32[]{:S(2)}) async-start(bf16[8,256,512]{1,2,0:T(8,128)(2,1)} %broadcast_in_dim.15), calls=%async_computation.1 | async-start | bytes 4194304 | tf_op jit(solution)/shard_map/all_to_all | solution.py:43
  361.5 2.0 copy-start.2
Sparse Core Ops, SparseCore 0:
  10.1 157.2 all-gather.3
  212.5 70.5 all-gather.5
  285.2 70.5 all-gather.7
